TPU v7x, 32 devices: a whole 2x2x4 slice. The times are simulated.
32 devices in a mesh: group: 2 (over x), wide: 16 (over z, y, core).
Axes of the slice: x: 2, y: 2, z: 4, core: 2. Of those that a mesh axis runs over, the one named last changes fastest.
Arguments:
- tokens: bfloat16 [192, 2688], P('group', 'wide'), parts along dimension 0, may hold values from -6 to 6
- mix_gain: bfloat16 [2688], replicated, may hold values from 0.099609375 to 1.8984375
- proj_inner: bfloat16 [2688, 2, 4096], P(None, None, 'wide'), may hold values from -0.125 to 0.125
- proj_maps: bfloat16 [2688, 2048], P(None, 'wide'), may hold values from -0.125 to 0.125
- proj_step: bfloat16 [2688, 64], P(None, 'wide'), may hold values from -0.125 to 0.125
- window_inner: bfloat16 [192, 3, 4096], P('group', None, 'wide'), parts along dimension 0, may hold values from -6 to 6
- window_maps: bfloat16 [192, 3, 2048], P('group', None, 'wide'), parts along dimension 0, may hold values from -6 to 6
- kernel_inner: bfloat16 [4, 4096], P(None, 'wide'), may hold values from -3 to 3
- kernel_maps: bfloat16 [4, 2048], P(None, 'wide'), may hold values from -3 to 3
- step_bias: float32 [64], P('wide'), may hold values from -4 to -1
- decay_log: float32 [64], P('wide'), may hold values from -1 to 2.5
- skip_gain: float32 [64], P('wide'), may hold values from 0.5 to 2
- gated_gain: bfloat16 [4096], P('wide'), may hold values from 0.099609375 to 1.8984375
- proj_out: bfloat16 [4096, 2688], P('wide'), may hold values from -0.125 to 0.125
- ssm_state: float32 [192, 64, 64, 128], P('group', 'wide'), parts along dimension 0, may hold values from -0.6 to 0.6
- moe_gain: bfloat16 [2688], replicated, may hold values from 0.099609375 to 1.8984375
- router_weight: bfloat16 [2688, 16], replicated, may hold values from -0.125 to 0.125
- expert_ids: int32 [192, 6], P('group'), parts along dimension 0, may hold values from 0 to 15, all different within a row; in each aligned block of 96 rows (0 to 95, 96 to 191, ...) at most 96 rows name the same one
- expert_up: bfloat16 [16, 2688, 928], P('wide'), may hold values from -0.125 to 0.125
- expert_down: bfloat16 [16, 928, 2688], P('wide'), may hold values from -0.1875 to 0.1875
Outputs:
- next_hidden: bfloat16 [192, 2688], P('group', 'wide'), parts along dimension 0
- new_state: float32 [192, 64, 64, 128], P('group', 'wide'), parts along dimension 0
There are 2 independent parts, one for each index of `group`. A program takes and returns all parts, laid end to end along the dimension named above; an argument that names none is the same for every part. Nothing has to cross between parts.
Inputs may be any that keep to these rules, and one draw needn't show every extreme that they name: `expert_ids`: each token names 6 different experts; no expert is named by more than 96 tokens of a part, a bound that some block reaches.
All inputs are finite; a program needn't handle non-finite values.
Results may differ from a plain program's by a relative error of at most 0.013.
Values may be sent and summed in bfloat16 or wider, within the bound.
A program may use at most 128 MiB of HBM per device.

v0:
```python
import jax
import jax.numpy as jnp
from jax import lax
from jax.sharding import PartitionSpec as P

WIDTH = 2688
HEADS = 64
HEAD_DIM = 64
STATE = 128
GROUPS = 8
TOPK = 6
INNER = 4096
epsilon = 1e-05


def rms_scale(values, axis):
    return lax.rsqrt(jnp.mean(values * values, axis=axis, keepdims=True) + epsilon)


def convolve(window, fresh, kernel):
    stacked = jnp.concatenate([window, fresh[:, None, :]], axis=1).astype(jnp.float32)
    mixed = jnp.sum(stacked * kernel.astype(jnp.float32)[None], axis=1)
    return jax.nn.silu(mixed).astype(jnp.bfloat16)


def expert_rows(rows, upward, downward):
    hidden_units = jnp.dot(rows, upward, preferred_element_type=jnp.float32)
    active = jnp.square(jnp.maximum(hidden_units, 0.0)).astype(jnp.bfloat16)
    return jnp.dot(active, downward, preferred_element_type=jnp.float32).astype(jnp.bfloat16)


def route_gates(logits, expert_ids):
    onehot = (
        expert_ids[:, :, None] == jnp.arange(logits.shape[1], dtype=jnp.int32)[None, None, :]
    ).astype(jnp.float32)
    chosen = jnp.sum(onehot * logits[:, None, :], axis=2)
    score = jax.nn.sigmoid(chosen)
    return score / jnp.sum(score, axis=1, keepdims=True)


def slot_codes(expert_ids, experts, capacity):
    flat = expert_ids.reshape(-1)
    onehot = (flat[:, None] == jnp.arange(experts, dtype=jnp.int32)[None, :]).astype(jnp.int32)
    before = jnp.cumsum(onehot, axis=0) - onehot
    slots = jnp.sum(before * onehot, axis=1)
    return (flat * capacity + slots).reshape(expert_ids.shape)


def slot_tables(codes, gates, count):
    targets = jnp.arange(count, dtype=jnp.int32)
    match = codes[None, :, :] == targets[:, None, None]
    pick = jnp.any(match, axis=2).astype(jnp.bfloat16)
    weigh = jnp.sum(jnp.where(match, gates[None], 0.0), axis=2)
    return (pick, weigh)


def local(
    tokens,
    mix_gain,
    proj_inner,
    proj_maps,
    proj_step,
    window_inner,
    window_maps,
    kernel_inner,
    kernel_maps,
    step_bias,
    decay_log,
    skip_gain,
    gated_gain,
    proj_out,
    ssm_state,
    moe_gain,
    router_weight,
    expert_ids,
    expert_up,
    expert_down,
):
    devices = lax.axis_size("wide")
    device = lax.axis_index("wide")
    seqs = tokens.shape[0]
    slice_width = tokens.shape[1]
    capacity = min(seqs, 4 * seqs * TOPK // devices)
    full_tokens = lax.all_gather(tokens, "wide", axis=1, tiled=True)
    tokens_float = full_tokens.astype(jnp.float32)
    normed = (tokens_float * rms_scale(tokens_float, 1) * mix_gain.astype(jnp.float32)).astype(
        jnp.bfloat16
    )
    local_inner = proj_inner.shape[2]
    inner = jnp.dot(
        normed, proj_inner.reshape(WIDTH, 2 * local_inner), preferred_element_type=jnp.float32
    ).astype(jnp.bfloat16)
    gate_input = inner[:, :local_inner]
    raw_inner = inner[:, local_inner:]
    maps_raw = jnp.dot(normed, proj_maps, preferred_element_type=jnp.float32).astype(jnp.bfloat16)
    step_raw = jnp.dot(normed, proj_step, preferred_element_type=jnp.float32).astype(jnp.bfloat16)
    conv_inner = convolve(window_inner, raw_inner, kernel_inner)
    conv_maps = convolve(window_maps, maps_raw, kernel_maps)
    all_maps = lax.all_gather(conv_maps, "wide", axis=1, tiled=True)
    local_heads = proj_step.shape[1]
    group = device * local_heads // (HEADS // GROUPS)
    in_maps = lax.dynamic_slice_in_dim(all_maps, group * STATE, STATE, 1).astype(jnp.float32)
    out_maps = lax.dynamic_slice_in_dim(all_maps, GROUPS * STATE + group * STATE, STATE, 1).astype(
        jnp.float32
    )
    step_size = jax.nn.softplus(step_raw.astype(jnp.float32) + step_bias)
    decay = jnp.exp(-jnp.exp(decay_log) * step_size)
    head_inputs = conv_inner.astype(jnp.float32).reshape(seqs, local_heads, HEAD_DIM)
    driven = (step_size[:, :, None] * head_inputs)[..., None] * in_maps[:, None, None, :]
    new_state = decay[:, :, None, None] * ssm_state + driven
    readout = (
        jnp.einsum("shpn,sn->shp", new_state, out_maps, precision=lax.Precision.HIGHEST)
        + skip_gain[None, :, None] * head_inputs
    )
    gated = readout.reshape(seqs, local_inner) * jax.nn.silu(gate_input.astype(jnp.float32))
    group_mask = (jnp.arange(GROUPS, dtype=jnp.int32) == group).astype(jnp.float32)
    partial_squares = jnp.sum(gated * gated, axis=1)[:, None] * group_mask[None, :]
    group_squares = lax.psum(partial_squares, "wide")
    own_squares = jnp.sum(group_squares * group_mask[None, :], axis=1, keepdims=True)
    norm_scale = lax.rsqrt(own_squares / (INNER // GROUPS) + epsilon)
    gated_out = (gated * norm_scale * gated_gain.astype(jnp.float32)).astype(jnp.bfloat16)
    mixer_terms = jnp.dot(gated_out, proj_out, preferred_element_type=jnp.float32)
    codes = slot_codes(expert_ids, devices, capacity)
    mixer_slice = lax.psum_scatter(mixer_terms, "wide", scatter_dimension=1, tiled=True)
    hidden_round = (tokens.astype(jnp.float32) + mixer_slice).astype(jnp.bfloat16)
    hidden_slice = lax.optimization_barrier(hidden_round).astype(jnp.float32)
    gain_slice = lax.dynamic_slice_in_dim(moe_gain, device * slice_width, slice_width, 0).astype(
        jnp.float32
    )
    router_slice = lax.dynamic_slice_in_dim(
        router_weight, device * slice_width, slice_width, 0
    ).astype(jnp.float32)
    weighted = hidden_slice * gain_slice
    squares, part_logits = lax.psum(
        (
            jnp.sum(hidden_slice * hidden_slice, axis=1),
            jnp.dot(weighted, router_slice, precision=lax.Precision.HIGHEST),
        ),
        "wide",
    )
    moe_scale = lax.rsqrt(squares[:, None] / WIDTH + epsilon)
    gates = route_gates(part_logits * moe_scale, expert_ids)
    moe_input = (hidden_slice * moe_scale * gain_slice).astype(jnp.bfloat16)
    pick, weigh = slot_tables(codes, gates, devices * capacity)
    sent = (
        jnp.dot(pick, moe_input, preferred_element_type=jnp.float32)
        .astype(jnp.bfloat16)
        .reshape(devices, capacity, slice_width)
    )
    served = expert_rows(
        lax.all_to_all(sent, "wide", split_axis=0, concat_axis=2, tiled=True)[0],
        expert_up[0],
        expert_down[0],
    )
    returned = lax.all_to_all(served[None], "wide", split_axis=2, concat_axis=0, tiled=True)
    moe_slice = jnp.dot(
        weigh.T,
        returned.reshape(devices * capacity, slice_width).astype(jnp.float32),
        precision=lax.Precision.HIGHEST,
    )
    next_hidden = (hidden_slice + moe_slice).astype(jnp.bfloat16)
    return (next_hidden, new_state)


def solution(mesh):
    in_specs = (
        P("group", "wide"),
        P(),
        P(None, None, "wide"),
        P(None, "wide"),
        P(None, "wide"),
        P("group", None, "wide"),
        P("group", None, "wide"),
        P(None, "wide"),
        P(None, "wide"),
        P("wide"),
        P("wide"),
        P("wide"),
        P("wide"),
        P("wide", None),
        P("group", "wide", None, None),
        P(),
        P(),
        P("group", None),
        P("wide", None, None),
        P("wide", None, None),
    )
    out_specs = (P("group", "wide"), P("group", "wide", None, None))
    return jax.shard_map(local, mesh=mesh, in_specs=in_specs, out_specs=out_specs, check_vma=False)
```

profile of v0, /device:TPU:0, one launch (start us, length us, event | category | flops | bytes accessed | tf_op | source)
XLA Modules:
  0.0 292.7 jit_solution(6536486973410003831)
XLA Ops:
  7.3 25.6 %all_gather.6 = bf16[96,2688]{0,1:T(8,128)(2,1)S(1)} all-gather(bf16[96,168]{0,1:T(8,128)(2,1)} %param.20), channel_id=1, replica_groups=mesh['group'=2,'wide'=16] {'wide'}, dimensions={1}, use_global_device_ids=true | all-gather | bytes 548352 | tf_op jit(solution)/shard_map/all_gather | solution.py:84
  32.9 0.4 fusion.11
  33.3 0.7 convert_element_type.109
  34.0 0.7 convert_element_type.120
  34.6 1.8 fusion.24
  36.6 18.5 %all_gather.7 = bf16[96,2048]{1,0:T(8,128)(2,1)S(1)} all-gather(bf16[96,128]{1,0:T(8,128)(2,1)S(1)} %multiply_convert_fusion.3), channel_id=1, replica_groups=mesh['group'=2,'wide'=16] {'wide'}, dimensions={1}, use_global_device_ids=true | all-gather | bytes 417792 | tf_op jit(solution)/shard_map/all_gather | solution.py:99
  55.1 0.5 copy.88
  55.6 1.2 convolution_convert_fusion.1
  56.9 0.1 copy.71
  57.0 0.5 multiply_exponential_fusion
  57.6 0.1 copy.72
  57.8 0.1 copy.70
  57.9 7.0 %multiply_add_fusion = f32[96,4,64,128]{3,2,1,0:T(8,128)S(1)} fusion(f32[96,4,64,128]{3,2,1,0:T(8,128)} %param.34, f32[96,128]{1,0:T(8,128)S(1)} %get-tuple-element.5, f32[96,4,64]{2,1,0:T(4,128)S(1)} %copy.72, f32[96,4]{1,0:T(8,128)S(1)} %copy.70), kind=kLoop, calls=%fused_computation | loop fusion | flops 9437184 | bytes 25314816 | tf_op jit(solution)/shard_map/add | solution.py:110
  64.9 4.8 %copy-done.1 = f32[96,4,64,128]{3,2,1,0:T(8,128)} copy-done((f32[96,4,64,128]{3,2,1,0:T(8,128)}, f32[96,4,64,128]{3,2,1,0:T(8,128)S(1)}, u32[]{:S(2)}) %copy-start.1) | copy-done | bytes 12582936
  69.7 14.7 %fusion.40 = f32[96,1,4,64]{3,1,2,0:T(1,128)S(1)} fusion(f32[96,4,64,128]{3,2,1,0:T(8,128)S(1)} %multiply_add_fusion, bf16[96,128,1,1]{1,0,2,3:T(8,128)(2,1)S(1)} %get-tuple-element.4), kind=kOutput, calls=%fused_computation.52 | convolution fusion | flops 37748736 | bytes 12705792 | tf_op jit(solution)/shard_map/shpn,sn->shp/dot_general | solution.py:112
  84.4 0.1 copy.84
  84.7 0.1 multiply_reduce_fusion.2
  84.9 31.1 %psum.21 = f32[96,8]{0,1:T(8,128)S(1)} all-reduce(f32[96,8]{0,1:T(8,128)S(1)} %broadcast_multiply_fusion.1), channel_id=1, replica_groups=mesh['group'=2,'wide'=16] {'wide'}, use_global_device_ids=true, to_apply=%region_4.5 | all-reduce | flops 768 | bytes 6144 | tf_op jit(solution)/shard_map/psum | solution.py:118
  116.1 1.8 fusion.39
  117.9 0.1 copy.74
  118.0 0.1 eq.60
  118.2 1.7 reduce-window.6
  119.9 0.2 slice_reduce_fusion
  120.2 0.1 reduce_sum.101
  120.4 0.8 dynamic-slice_convert_fusion.1
  121.2 0.6 fusion.4
  121.9 50.8 %reduce-scatter.4.cloned.1.call-done = f32[96,168]{0,1:T(8,128)} async-done(((f32[96,2688]{0,1:T(8,128)}), f32[96,168]{0,1:T(8,128)}) %reduce-scatter.4.cloned.1.call-update) | async-done | bytes 64528
  172.7 0.9 add_convert_fusion
  173.6 0.9 fusion.35
  174.5 30.5 %all-reduce.2 = (f32[96,16]{0,1:T(8,128)S(1)}, f32[96]{0:T(128)S(1)}) all-reduce(f32[96,16]{0,1:T(8,128)S(1)} %fusion.35, f32[96]{0:T(128)S(1)} %fusion.36), channel_id=1, replica_groups=mesh['group'=2,'wide'=16] {'wide'}, use_global_device_ids=true, to_apply=%region_10.11 | all-reduce | flops 1632 | bytes 13056 | tf_op jit(solution)/shard_map/psum | solution.py:134
  205.0 0.3 convolution_convert_fusion
  205.4 0.6 reshape.115
  205.9 0.2 copy.78
  206.1 21.2 %all_to_all.30 = bf16[16,96,168]{1,2,0:T(8,128)(2,1)S(1)} all-to-all(bf16[16,96,168]{1,2,0:T(8,128)(2,1)S(1)} %copy.78), channel_id=1, replica_groups=mesh['group'=2,'wide'=16] {'wide'}, dimensions={0} | all-to-all | bytes 1032192 | tf_op jit(solution)/shard_map/all_to_all | solution.py:151
  227.4 6.5 %fusion.8 = bf16[1,96,2688]{2,1,0:T(8,128)(2,1)S(1)} fusion(bf16[1,928,2688]{2,1,0:T(8,128)(2,1)} %param.39, bf16[96,2688]{0,1:T(8,128)(2,1)S(1)} %bitcast.74, bf16[1,2688,928]{1,2,0:T(8,128)(2,1)} %param.38), kind=kOutput, calls=%fused_computation.9 | convolution fusion | flops 958399488 | bytes 11010048 | tf_op jit(solution)/shard_map/dot_general | solution.py:29
  233.9 1.9 copy.80
  235.8 0.5 broadcast.123
  236.3 14.9 %reduce.2 = bf16[2688,96]{1,0:T(8,128)(2,1)S(1)} reduce(bf16[2688,1,96]{2,1,0:T(2,128)(2,1)S(1)} %bitcast.70, bf16[]{:T(256)} %broadcast.123), dimensions={1}, to_apply=%bitcast.55.reduce_sub_computation | reduce | bytes 1032194
  251.3 1.9 reshape.122
  253.2 4.5 %all-to-all-start.1 = ((bf16[16,2,8064]{2,1,0:T(2,128)(2,1)}), bf16[16,2,8064]{2,1,0:T(2,128)(2,1)}, u32[]{:S(2)}, u32[]{:S(2)}) async-start(bf16[16,2,8064]{2,1,0:T(2,128)(2,1)} %reshape.122), calls=%async_computation.1 | async-start | bytes 1032192 | tf_op jit(solution)/shard_map/all_to_all | solution.py:155
  257.8 0.5 select_reduce_fusion
  258.3 13.3 %all-to-all-done.1 = bf16[16,2,8064]{2,1,0:T(2,128)(2,1)} async-done(((bf16[16,2,8064]{2,1,0:T(2,128)(2,1)}), bf16[16,2,8064]{2,1,0:T(2,128)(2,1)}, u32[]{:S(2)}, u32[]{:S(2)}) %all-to-all-start.1) | async-done | bytes 516128 | tf_op jit(solution)/shard_map/all_to_all | solution.py:155
  271.6 5.0 %reshape.123 = bf16[2688,1,96]{2,1,0:T(2,128)(2,1)S(1)} reshape(bf16[16,2,8064]{2,1,0:T(2,128)(2,1)} %all-to-all-done.1) | data formatting | bytes 1032192
  276.6 2.8 copy.81
  279.4 3.3 %all_to_all.26 = bf16[1,96,16,168]{3,2,1,0:T(8,128)(2,1)S(1)} reshape(bf16[1,96,2688]{2,1,0:T(8,128)(2,1)} %copy.81) | data formatting | bytes 1032192 | tf_op jit(solution)/shard_map/all_to_all | solution.py:155
  282.7 1.2 copy.82
  283.9 0.7 reshape.116
  284.6 1.2 fusion.23
  (56 shorter events, 1.0 us)
Async XLA Ops:
  7.2 108.9 %copy-start = (bf16[256,2688]{1,0:T(8,128)(2,1)S(1)}, bf16[256,2688]{1,0:T(8,128)(2,1)}, u32[]{:S(2)}) copy-start(bf16[256,2688]{1,0:T(8,128)(2,1)} %param.33) | copy-start | bytes 4128772
  7.2 29.3 %copy-start.5 = (bf16[96,3,128]{2,0,1:T(8,128)(2,1)S(1)}, bf16[96,3,128]{2,0,1:T(8,128)(2,1)}, u32[]{:S(2)}) copy-start(bf16[96,3,128]{2,0,1:T(8,128)(2,1)} %param.26) | copy-start | bytes 221188
  7.2 165.5 %reduce-scatter.4.cloned.1.call-start = ((), (), s32[]{:S(2)}) async-start(), calls=%async_computation.3 | async-start | bytes 1462272
  7.3 47.8 %copy-start.2 = (bf16[2688,2,256]{2,1,0:T(2,128)(2,1)S(1)}, bf16[2688,2,256]{2,1,0:T(2,128)(2,1)}, u32[]{:S(2)}) copy-start(bf16[2688,2,256]{2,1,0:T(2,128)(2,1)} %param.22) | copy-start | bytes 8257540
  55.5 1.3 copy-start.7
  55.6 1.3 copy-start.4
  55.6 1.4 copy-start.10
  55.6 1.4 copy-start.9
  55.6 1.4 copy-start.11
  64.9 4.8 %copy-start.1 = (f32[96,4,64,128]{3,2,1,0:T(8,128)}, f32[96,4,64,128]{3,2,1,0:T(8,128)S(1)}, u32[]{:S(2)}) copy-start(f32[96,4,64,128]{3,2,1,0:T(8,128)S(1)} %multiply_add_fusion) | copy-start | bytes 37748740
  69.7 14.8 %copy-start.8 = (f32[4]{0:T(128)S(1)}, f32[4]{0:T(128)}, u32[]{:S(2)}) copy-start(f32[4]{0:T(128)} %param.31) | copy-start | bytes 52
  69.7 46.4 %copy-start.12 = (bf16[256]{0:T(256)(128)(2,1)S(1)}, bf16[256]{0:T(256)(128)(2,1)}, u32[]{:S(2)}) copy-start(bf16[256]{0:T(256)(128)(2,1)} %param.32) | copy-start | bytes 1540
  84.4 33.6 %copy-start.6 = (s32[96,6]{0,1:T(8,128)S(1)}, s32[96,6]{0,1:T(8,128)}, u32[]{:S(2)}) copy-start(s32[96,6]{0,1:T(8,128)} %param.37) | copy-start | bytes 6916
  84.6 88.1 %copy-start.3 = (bf16[96,168]{0,1:T(8,128)(2,1)S(1)}, bf16[96,168]{0,1:T(8,128)(2,1)}, u32[]{:S(2)}) copy-start(bf16[96,168]{0,1:T(8,128)(2,1)} %param.20) | copy-start | bytes 96772
  253.2 18.4 %all-to-all-start.1 = ((bf16[16,2,8064]{2,1,0:T(2,128)(2,1)}), bf16[16,2,8064]{2,1,0:T(2,128)(2,1)}, u32[]{:S(2)}, u32[]{:S(2)}) async-start(bf16[16,2,8064]{2,1,0:T(2,128)(2,1)} %reshape.122), calls=%async_computation.1 | async-start | bytes 1032192 | tf_op jit(solution)/shard_map/all_to_all | solution.py:155
Sparse Core Ops, SparseCore 0:
  118.0 54.5 reduce-scatter.3
where the time goes:
time: 293 us
  blocking collectives  127 us (43%)
  waiting for transfers between devices  64.1 us (22%)
  other arithmetic  29 us (10%)
  matrix products  29 us (10%)
  local copies, waits for them, and re-layouts  24.6 us (8%)
  between operations  14.5 us (5%)
  starting transfers between devices  4.53 us (2%)
    unnamed x2, waiting for transfers between devices  50.8 us
    psum x1, blocking collectives, local(): group_squares = lax.psum(partial_squares, 'wide')  31.1 us
    psum x1, blocking collectives, local(): lax.psum((jnp.sum(hidden_slice * hidden_slice, axis=1), jnp.dot(weighted,...  30.5 us
    all_gather x1, blocking collectives, local(): full_tokens = lax.all_gather(tokens, 'wide', axis=1, tiled=True)  25.6 us
    all_to_all x1, blocking collectives, local(): lax.all_to_all(sent, 'wide', split_axis=0, concat_axis=2, tiled=True)[0]  21.2 us
    all_gather x1, blocking collectives, local(): all_maps = lax.all_gather(conv_maps, 'wide', axis=1, tiled=True)  18.5 us
    unnamed x1, other arithmetic  14.9 us
    dot_general x1, matrix products, local(): jnp.einsum('shpn,sn->shp', new_state, out_maps, precision=lax.Precision.H...  14.7 us
  transfers between devices with their start and end apart: 2, of which 2 were waited for; matrix products, arithmetic and copies ran while one was open for 2% of the time, Pallas kernels for 0%

commit v1 on v0

--- a/solution.py
+++ b/solution.py
@@ -115,7 +115,7 @@
     gated = readout.reshape(seqs, local_inner) * jax.nn.silu(gate_input.astype(jnp.float32))
     group_mask = (jnp.arange(GROUPS, dtype=jnp.int32) == group).astype(jnp.float32)
     partial_squares = jnp.sum(gated * gated, axis=1)[:, None] * group_mask[None, :]
-    group_squares = lax.psum(partial_squares, "wide")
+    group_squares = jnp.sum(lax.all_gather(partial_squares, "wide"), axis=0)
     own_squares = jnp.sum(group_squares * group_mask[None, :], axis=1, keepdims=True)
     norm_scale = lax.rsqrt(own_squares / (INNER // GROUPS) + epsilon)
     gated_out = (gated * norm_scale * gated_gain.astype(jnp.float32)).astype(jnp.bfloat16)

time: 293 us -> 281 us (0.959)
  blocking collectives: 127 us -> 115 us
    psum x1 -> x0, blocking collectives: 31.1 us -> none  [local(): group_squares = lax.psum(partial_squares, 'wide')]
    all_gather x0 -> x1, blocking collectives: none -> 18.9 us  [local(): group_squares = jnp.sum(lax.all_gather(partial_squares, 'wide'), axis=0)]
where the time goes in v1:
time: 281 us
  blocking collectives  115 us (41%)
  waiting for transfers between devices  64.1 us (23%)
  other arithmetic  29 us (10%)
  matrix products  29 us (10%)
  local copies, waits for them, and re-layouts  24.6 us (9%)
  between operations  14.5 us (5%)
  starting transfers between devices  4.53 us (2%)
    unnamed x2, waiting for transfers between devices  50.8 us
    psum x1, blocking collectives, local(): lax.psum((jnp.sum(hidden_slice * hidden_slice, axis=1), jnp.dot(weighted,...  30.5 us
    all_gather x1, blocking collectives, local(): full_tokens = lax.all_gather(tokens, 'wide', axis=1, tiled=True)  25.6 us
    all_to_all x1, blocking collectives, local(): lax.all_to_all(sent, 'wide', split_axis=0, concat_axis=2, tiled=True)[0]  21.2 us
    all_gather x1, blocking collectives, local(): group_squares = jnp.sum(lax.all_gather(partial_squares, 'wide'), axis=0)  18.9 us
    all_gather x1, blocking collectives, local(): all_maps = lax.all_gather(conv_maps, 'wide', axis=1, tiled=True)  18.5 us
    unnamed x1, other arithmetic  14.9 us
    dot_general x1, matrix products, local(): jnp.einsum('shpn,sn->shp', new_state, out_maps, precision=lax.Precision.H...  14.7 us
  transfers between devices with their start and end apart: 2, of which 2 were waited for; matrix products, arithmetic and copies ran while one was open for 2% of the time, Pallas kernels for 0%

profile of v1, /device:TPU:0, one launch (start us, length us, event | category | flops | bytes accessed | tf_op | source)
XLA Modules:
  0.0 280.5 jit_solution(15201347027252152062)
XLA Ops:
  7.3 25.6 %all_gather.10 = bf16[96,2688]{0,1:T(8,128)(2,1)S(1)} all-gather(bf16[96,168]{0,1:T(8,128)(2,1)} %param.20), channel_id=1, replica_groups=mesh['group'=2,'wide'=16] {'wide'}, dimensions={1}, use_global_device_ids=true | all-gather | bytes 548352 | tf_op jit(solution)/shard_map/all_gather | solution.py:84
  32.9 0.4 fusion.11
  33.3 0.7 convert_element_type.109
  34.0 0.7 convert_element_type.120
  34.6 1.8 fusion.24
  36.6 18.5 %all_gather.11 = bf16[96,2048]{1,0:T(8,128)(2,1)S(1)} all-gather(bf16[96,128]{1,0:T(8,128)(2,1)S(1)} %multiply_convert_fusion.3), channel_id=1, replica_groups=mesh['group'=2,'wide'=16] {'wide'}, dimensions={1}, use_global_device_ids=true | all-gather | bytes 417792 | tf_op jit(solution)/shard_map/all_gather | solution.py:99
  55.1 0.5 copy.104
  55.6 1.2 convolution_convert_fusion.1
  56.9 0.1 copy.87
  57.0 0.5 multiply_exponential_fusion
  57.6 0.1 copy.88
  57.8 0.1 copy.86
  57.9 7.0 %multiply_add_fusion = f32[96,4,64,128]{3,2,1,0:T(8,128)S(1)} fusion(f32[96,4,64,128]{3,2,1,0:T(8,128)} %param.34, f32[96,128]{1,0:T(8,128)S(1)} %get-tuple-element.5, f32[96,4,64]{2,1,0:T(4,128)S(1)} %copy.88, f32[96,4]{1,0:T(8,128)S(1)} %copy.86), kind=kLoop, calls=%fused_computation | loop fusion | flops 9437184 | bytes 25314816 | tf_op jit(solution)/shard_map/add | solution.py:110
  64.9 4.8 %copy-done.1 = f32[96,4,64,128]{3,2,1,0:T(8,128)} copy-done((f32[96,4,64,128]{3,2,1,0:T(8,128)}, f32[96,4,64,128]{3,2,1,0:T(8,128)S(1)}, u32[]{:S(2)}) %copy-start.1) | copy-done | bytes 12582936
  69.7 14.7 %fusion.40 = f32[96,1,4,64]{3,1,2,0:T(1,128)S(1)} fusion(f32[96,4,64,128]{3,2,1,0:T(8,128)S(1)} %multiply_add_fusion, bf16[96,128,1,1]{1,0,2,3:T(8,128)(2,1)S(1)} %get-tuple-element.4), kind=kOutput, calls=%fused_computation.52 | convolution fusion | flops 37748736 | bytes 12705792 | tf_op jit(solution)/shard_map/shpn,sn->shp/dot_general | solution.py:112
  84.4 0.1 copy.100
  84.7 0.1 multiply_reduce_fusion.2
  84.9 18.9 %all_gather.12 = f32[16,96,8]{1,2,0:T(8,128)S(1)} all-gather(f32[1,96,8]{1,2,0:T(8,128)S(1)} %broadcast_multiply_fusion.1), channel_id=1, replica_groups=mesh['group'=2,'wide'=16] {'wide'}, dimensions={0}, use_global_device_ids=true | all-gather | bytes 52224 | tf_op jit(solution)/shard_map/all_gather | solution.py:118
  104.0 1.8 fusion.39
  105.8 0.1 copy.90
  105.9 0.1 eq.60
  106.1 1.7 reduce-window.6
  107.7 0.2 slice_reduce_fusion
  108.1 0.1 reduce_sum.111
  108.3 0.8 dynamic-slice_convert_fusion.1
  109.1 0.6 fusion.4
  109.7 50.8 %reduce-scatter.4.cloned.1.call-done = f32[96,168]{0,1:T(8,128)} async-done(((f32[96,2688]{0,1:T(8,128)}), f32[96,168]{0,1:T(8,128)}) %reduce-scatter.4.cloned.1.call-update) | async-done | bytes 64528
  160.5 0.9 add_convert_fusion
  161.4 0.9 fusion.35
  162.3 30.5 %all-reduce.2 = (f32[96,16]{0,1:T(8,128)S(1)}, f32[96]{0:T(128)S(1)}) all-reduce(f32[96,16]{0,1:T(8,128)S(1)} %fusion.35, f32[96]{0:T(128)S(1)} %fusion.36), channel_id=1, replica_groups=mesh['group'=2,'wide'=16] {'wide'}, use_global_device_ids=true, to_apply=%region_10.11 | all-reduce | flops 1632 | bytes 13056 | tf_op jit(solution)/shard_map/psum | solution.py:134
  192.8 0.3 convolution_convert_fusion
  193.2 0.6 reshape.156
  193.8 0.2 copy.94
  193.9 21.2 %all_to_all.30 = bf16[16,96,168]{1,2,0:T(8,128)(2,1)S(1)} all-to-all(bf16[16,96,168]{1,2,0:T(8,128)(2,1)S(1)} %copy.94), channel_id=1, replica_groups=mesh['group'=2,'wide'=16] {'wide'}, dimensions={0} | all-to-all | bytes 1032192 | tf_op jit(solution)/shard_map/all_to_all | solution.py:151
  215.2 6.5 %fusion.8 = bf16[1,96,2688]{2,1,0:T(8,128)(2,1)S(1)} fusion(bf16[1,928,2688]{2,1,0:T(8,128)(2,1)} %param.39, bf16[96,2688]{0,1:T(8,128)(2,1)S(1)} %bitcast.74, bf16[1,2688,928]{1,2,0:T(8,128)(2,1)} %param.38), kind=kOutput, calls=%fused_computation.9 | convolution fusion | flops 958399488 | bytes 11010048 | tf_op jit(solution)/shard_map/dot_general | solution.py:29
  221.7 1.9 copy.96
  223.6 0.5 broadcast.159
  224.2 14.9 %reduce.2 = bf16[2688,96]{1,0:T(8,128)(2,1)S(1)} reduce(bf16[2688,1,96]{2,1,0:T(2,128)(2,1)S(1)} %bitcast.70, bf16[]{:T(256)} %broadcast.159), dimensions={1}, to_apply=%bitcast.55.reduce_sub_computation | reduce | bytes 1032194
  239.1 1.9 reshape.163
  241.0 4.5 %all-to-all-start.1 = ((bf16[16,2,8064]{2,1,0:T(2,128)(2,1)}), bf16[16,2,8064]{2,1,0:T(2,128)(2,1)}, u32[]{:S(2)}, u32[]{:S(2)}) async-start(bf16[16,2,8064]{2,1,0:T(2,128)(2,1)} %reshape.163), calls=%async_computation.1 | async-start | bytes 1032192 | tf_op jit(solution)/shard_map/all_to_all | solution.py:155
  245.6 0.5 select_reduce_fusion
  246.1 13.3 %all-to-all-done.1 = bf16[16,2,8064]{2,1,0:T(2,128)(2,1)} async-done(((bf16[16,2,8064]{2,1,0:T(2,128)(2,1)}), bf16[16,2,8064]{2,1,0:T(2,128)(2,1)}, u32[]{:S(2)}, u32[]{:S(2)}) %all-to-all-start.1) | async-done | bytes 516128 | tf_op jit(solution)/shard_map/all_to_all | solution.py:155
  259.4 5.0 %reshape.164 = bf16[2688,1,96]{2,1,0:T(2,128)(2,1)S(1)} reshape(bf16[16,2,8064]{2,1,0:T(2,128)(2,1)} %all-to-all-done.1) | data formatting | bytes 1032192
  264.4 2.8 copy.97
  267.2 3.3 %all_to_all.26 = bf16[1,96,16,168]{3,2,1,0:T(8,128)(2,1)S(1)} reshape(bf16[1,96,2688]{2,1,0:T(8,128)(2,1)} %copy.97) | data formatting | bytes 1032192 | tf_op jit(solution)/shard_map/all_to_all | solution.py:155
  270.5 1.2 copy.98
  271.7 0.7 reshape.157
  272.4 1.2 fusion.23
  (57 shorter events, 1.0 us)
Async XLA Ops:
  7.2 96.8 %copy-start = (bf16[256,2688]{1,0:T(8,128)(2,1)S(1)}, bf16[256,2688]{1,0:T(8,128)(2,1)}, u32[]{:S(2)}) copy-start(bf16[256,2688]{1,0:T(8,128)(2,1)} %param.33) | copy-start | bytes 4128772
  7.2 29.3 %copy-start.5 = (bf16[96,3,128]{2,0,1:T(8,128)(2,1)S(1)}, bf16[96,3,128]{2,0,1:T(8,128)(2,1)}, u32[]{:S(2)}) copy-start(bf16[96,3,128]{2,0,1:T(8,128)(2,1)} %param.26) | copy-start | bytes 221188
  7.2 153.3 %reduce-scatter.4.cloned.1.call-start = ((), (), s32[]{:S(2)}) async-start(), calls=%async_computation.3 | async-start | bytes 1462272
  7.3 47.8 %copy-start.2 = (bf16[2688,2,256]{2,1,0:T(2,128)(2,1)S(1)}, bf16[2688,2,256]{2,1,0:T(2,128)(2,1)}, u32[]{:S(2)}) copy-start(bf16[2688,2,256]{2,1,0:T(2,128)(2,1)} %param.22) | copy-start | bytes 8257540
  55.5 1.3 copy-start.7
  55.6 1.3 copy-start.4
  55.6 1.4 copy-start.10
  55.6 1.4 copy-start.9
  55.6 1.4 copy-start.11
  64.9 4.8 %copy-start.1 = (f32[96,4,64,128]{3,2,1,0:T(8,128)}, f32[96,4,64,128]{3,2,1,0:T(8,128)S(1)}, u32[]{:S(2)}) copy-start(f32[96,4,64,128]{3,2,1,0:T(8,128)S(1)} %multiply_add_fusion) | copy-start | bytes 37748740
  69.7 14.8 %copy-start.8 = (f32[4]{0:T(128)S(1)}, f32[4]{0:T(128)}, u32[]{:S(2)}) copy-start(f32[4]{0:T(128)} %param.31) | copy-start | bytes 52
  69.7 34.3 %copy-start.12 = (bf16[256]{0:T(256)(128)(2,1)S(1)}, bf16[256]{0:T(256)(128)(2,1)}, u32[]{:S(2)}) copy-start(bf16[256]{0:T(256)(128)(2,1)} %param.32) | copy-start | bytes 1540
  84.4 21.4 %copy-start.6 = (s32[96,6]{0,1:T(8,128)S(1)}, s32[96,6]{0,1:T(8,128)}, u32[]{:S(2)}) copy-start(s32[96,6]{0,1:T(8,128)} %param.37) | copy-start | bytes 6916
  84.6 75.9 %copy-start.3 = (bf16[96,168]{0,1:T(8,128)(2,1)S(1)}, bf16[96,168]{0,1:T(8,128)(2,1)}, u32[]{:S(2)}) copy-start(bf16[96,168]{0,1:T(8,128)(2,1)} %param.20) | copy-start | bytes 96772
  241.0 18.4 %all-to-all-start.1 = ((bf16[16,2,8064]{2,1,0:T(2,128)(2,1)}), bf16[16,2,8064]{2,1,0:T(2,128)(2,1)}, u32[]{:S(2)}, u32[]{:S(2)}) async-start(bf16[16,2,8064]{2,1,0:T(2,128)(2,1)} %reshape.163), calls=%async_computation.1 | async-start | bytes 1032192 | tf_op jit(solution)/shard_map/all_to_all | solution.py:155
Sparse Core Ops, SparseCore 0:
  105.9 54.5 reduce-scatter.3
